TPU v7x, 32 devices: a whole 2x2x4 slice. The times are simulated.
32 devices in a mesh: rep: 4 (over y, x), shard: 8 (over z, core).
Axes of the slice: x: 2, y: 2, z: 4, core: 2. Of those that a mesh axis runs over, the one named last changes fastest.
Arguments:
- tokens: bfloat16 [4096, 768], P(('rep', 'shard')), may hold values from -6 to 6
- segment_ids: int32 [32, 128], P(('rep', 'shard')), may hold values from 0 to 3, never falling along the last dimension, each value on 1 to 64 neighbouring positions
- first_gain: bfloat16 [768], P('shard'), may hold values from 0.5 to 1.5
- first_shift: bfloat16 [768], P('shard'), may hold values from -3 to 3
- qkv_weight: bfloat16 [768, 2304], P('shard'), may hold values from -3 to 3, as said below
- qv_bias: bfloat16 [2, 768], P(None, 'shard'), may hold values from -3 to 3
- proj_weight: bfloat16 [768, 768], P('shard'), may hold values from -0.625 to 0.625
- proj_bias: bfloat16 [768], P('shard'), may hold values from -3 to 3
- second_gain: bfloat16 [768], P('shard'), may hold values from 0.5 to 1.5
- second_shift: bfloat16 [768], P('shard'), may hold values from -3 to 3
- fc_weight: bfloat16 [768, 3072], P('shard'), may hold values from -0.21875 to 0.21875
- fc_bias: bfloat16 [3072], P('shard'), may hold values from -3 to 3
- out_weight: bfloat16 [3072, 768], P('shard'), may hold values from -0.109375 to 0.109375
- out_bias: bfloat16 [768], P('shard'), may hold values from -3 to 3
- cotangent: bfloat16 [4096, 768], P(('rep', 'shard')), may hold values from -6 to 6
Outputs:
- block_output: bfloat16 [4096, 768], P(('rep', 'shard'))
- grad_tokens: float32 [4096, 768], P(('rep', 'shard'))
- grad_first_gain: float32 [768], P('shard')
- grad_first_shift: float32 [768], P('shard')
- grad_qkv_weight: float32 [768, 2304], P('shard')
- grad_qv_bias: float32 [2, 768], P(None, 'shard')
- grad_proj_weight: float32 [768, 768], P('shard')
- grad_proj_bias: float32 [768], P('shard')
- grad_second_gain: float32 [768], P('shard')
- grad_second_shift: float32 [768], P('shard')
- grad_fc_weight: float32 [768, 3072], P('shard')
- grad_fc_bias: float32 [3072], P('shard')
- grad_out_weight: float32 [3072, 768], P('shard')
- grad_out_bias: float32 [768], P('shard')
Inputs may be any that keep to these rules, and one draw needn't show every extreme that they name: `segment_ids`: each row holds 4 runs of equal numbers in rising order, each run 1 to 64 long, one of them exactly 64. `qkv_weight`: columns 0 to 767 project to queries, the next 768 columns to keys, the last 768 columns to values.
All inputs are finite; a program needn't handle non-finite values.
Results may differ from a plain program's by a relative error of at most 0.011.
Values may be sent and summed in bfloat16 or wider, within the bound.
A program may use at most 128 MiB of HBM per device.

v0:
```python
import math
import jax
import jax.numpy as jnp
from jax import lax
from jax.sharding import PartitionSpec as P

D = 768
HEADS = 12
HD = 64
FF = 3072
EPSILON = 1e-05


def layer_norm(field, norm_gain, norm_shift):
    center = field - jnp.mean(field, axis=-1, keepdims=True)
    spread = jnp.mean(center * center, axis=-1, keepdims=True)
    return center * lax.rsqrt(spread + EPSILON) * norm_gain + norm_shift


def gelu_tanh(field):
    return jax.nn.gelu(field, approximate=True)


def head_split(matrix):
    return matrix.reshape(matrix.shape[0], HEADS, HD)


def masked_scores(query, keys, segments):
    rows = query.shape[0]
    scores = jnp.einsum(
        "qhd,khd->hqk", head_split(query), head_split(keys), preferred_element_type=jnp.float32
    ) * (1.0 / math.sqrt(HD))
    position = lax.iota(jnp.int32, rows)
    allowed = (segments[:, None] == segments[None, :]) & (position[None, :] <= position[:, None])
    return jnp.where(allowed[None], scores, -1e30)


def attend_forward(query, keys, values, segments):
    rows = query.shape[0]
    scores = masked_scores(query, keys, segments)
    row_max = jnp.max(scores, axis=-1, keepdims=True)
    row_total = jnp.sum(jnp.exp(scores - row_max), axis=-1, keepdims=True)
    logsum = row_max + jnp.log(row_total)
    probs = jnp.exp(scores - logsum).astype(jnp.bfloat16)
    attended = jnp.einsum(
        "hqk,khd->qhd", probs, head_split(values), preferred_element_type=jnp.float32
    )
    return (attended.reshape(rows, D).astype(jnp.bfloat16), logsum)


def attend_backward(query, keys, values, segments, attended, logsum, grad_attended):
    rows = query.shape[0]
    scores = masked_scores(query, keys, segments)
    weights = jnp.exp(scores - logsum)
    grad_heads = head_split(grad_attended)
    grad_values = jnp.einsum(
        "hqk,qhd->khd", weights.astype(jnp.bfloat16), grad_heads, preferred_element_type=jnp.float32
    )
    grad_probs = jnp.einsum(
        "qhd,khd->hqk", grad_heads, head_split(values), preferred_element_type=jnp.float32
    )
    delta = jnp.einsum(
        "qhd,qhd->hq", grad_heads, head_split(attended), preferred_element_type=jnp.float32
    )
    grad_scores = (weights * (grad_probs - delta[..., None]) * (1.0 / math.sqrt(HD))).astype(
        jnp.bfloat16
    )
    grad_query = jnp.einsum(
        "hqk,khd->qhd", grad_scores, head_split(keys), preferred_element_type=jnp.float32
    )
    grad_keys = jnp.einsum(
        "hqk,qhd->khd", grad_scores, head_split(query), preferred_element_type=jnp.float32
    )
    return (grad_query.reshape(rows, D), grad_keys.reshape(rows, D), grad_values.reshape(rows, D))


def exchange(field, axis, split, concat):
    return lax.all_to_all(field, axis, split_axis=split, concat_axis=concat, tiled=True)


def spread(field, axis):
    parts = lax.axis_size(axis)
    return exchange(jnp.broadcast_to(field[None], (parts,) + field.shape), axis, 0, 0)


def by_replica(field, shards, reps):
    rows = field.shape[0]
    return field.reshape(shards, reps, rows // (shards * reps), -1).swapaxes(0, 1).reshape(rows, -1)


def per_device(
    tokens,
    segment_ids,
    first_gain,
    first_shift,
    qkv_weight,
    qv_bias,
    proj_weight,
    proj_bias,
    second_gain,
    second_shift,
    fc_weight,
    fc_bias,
    out_weight,
    out_bias,
    cotangent,
):
    low = jnp.bfloat16
    segments = segment_ids[0]
    own_rows = tokens.shape[0]
    shards = lax.axis_size("shard")
    reps = lax.axis_size("rep")
    factor = 1.0 / math.sqrt(own_rows * reps * shards)
    small = jnp.stack(
        [
            first_gain,
            first_shift,
            qv_bias[0],
            qv_bias[1],
            proj_bias,
            second_gain,
            second_shift,
            out_bias,
        ]
    )
    small_full = lax.all_gather(small, "shard", axis=1, tiled=True).astype(jnp.float32)
    gain_one, shift_one, q_bias, v_bias, proj_bias_full, gain_two, shift_two, out_bias_full = (
        small_full[i] for i in range(8)
    )
    qkv_full = lax.all_gather(qkv_weight, "shard", axis=0, tiled=True)
    proj_full = lax.all_gather(proj_weight, "shard", axis=0, tiled=True)
    fc_cols = exchange(fc_weight, "shard", 1, 0)
    inputs = tokens.astype(jnp.float32)
    normed_f, first_back = jax.vjp(layer_norm, inputs, gain_one, shift_one)
    normed_first = normed_f.astype(low)
    projected = jnp.dot(normed_first, qkv_full, preferred_element_type=jnp.float32)
    query = (projected[:, :D] + q_bias).astype(low)
    keys = projected[:, D : 2 * D].astype(low)
    values = (projected[:, 2 * D :] + v_bias).astype(low)
    attended, logsum = attend_forward(query, keys, values, segments)
    residual = (
        inputs + jnp.dot(attended, proj_full, preferred_element_type=jnp.float32) + proj_bias_full
    )
    cot_f = cotangent.astype(jnp.float32)
    normed_s, second_back = jax.vjp(layer_norm, residual, gain_two, shift_two)
    normed_all = lax.all_gather(normed_s.astype(low), "shard", axis=0, tiled=True)
    cot_later, normed_all = lax.optimization_barrier((cotangent, normed_all))
    cot_all = lax.all_gather(cot_later, "shard", axis=0, tiled=True)
    pre_act = jnp.dot(normed_all, fc_cols, preferred_element_type=jnp.float32) + fc_bias.astype(
        jnp.float32
    )
    activated, gelu_back = jax.vjp(gelu_tanh, pre_act)
    hidden = activated.astype(low)
    grad_hidden = jnp.dot(cot_all, out_weight.T, preferred_element_type=jnp.float32)
    (grad_pre,) = gelu_back(grad_hidden)
    grad_pre_low = grad_pre.astype(low)
    grad_normed_part = jnp.dot(grad_pre_low, fc_cols.T, preferred_element_type=jnp.float32).astype(
        low
    )
    grad_normed_low = lax.psum_scatter(grad_normed_part, "shard", scatter_dimension=0, tiled=True)
    term_out_weight = jnp.dot(hidden.T, cot_all, preferred_element_type=jnp.float32) * factor
    term_fc_weight = (
        jnp.dot(normed_all.T, grad_pre_low, preferred_element_type=jnp.float32) * factor
    )
    out_part = jnp.dot(hidden, out_weight, preferred_element_type=jnp.float32).astype(low)
    ff_terms = jnp.concatenate(
        [
            term_out_weight.astype(low).reshape(reps, -1, D),
            by_replica(term_fc_weight.astype(low), shards, reps).reshape(reps, -1, D),
        ],
        axis=1,
    )
    ff_sum = jnp.sum(exchange(ff_terms, "rep", 0, 0).astype(jnp.float32), axis=0).astype(low)
    first_later, attended_later, grad_normed_low, ff_sum = lax.optimization_barrier(
        (normed_first, attended, grad_normed_low, ff_sum)
    )
    first_all = lax.all_gather(first_later, "shard", axis=0, tiled=True)
    grad_normed_second = grad_normed_low.astype(jnp.float32)
    grad_from_norm, second_gain_sum, second_shift_sum = second_back(grad_normed_second)
    grad_residual = cot_f + grad_from_norm
    grad_residual_low = grad_residual.astype(low)
    grad_residual_all = lax.all_gather(grad_residual_low, "shard", axis=0, tiled=True)
    attended_cols = exchange(attended_later, "shard", 1, 0)
    grad_attended = jnp.dot(
        grad_residual_low, proj_full.T, preferred_element_type=jnp.float32
    ).astype(low)
    out_rows = out_weight.shape[0] // reps
    out_piece = ff_sum[:out_rows]
    fc_piece = ff_sum[out_rows:].reshape(D // reps, -1)
    fc_piece = exchange(fc_piece, "shard", 0, 1)
    ff_all = spread(jnp.concatenate([out_piece, fc_piece.reshape(-1, D)]), "rep").astype(
        jnp.float32
    )
    grad_query, grad_keys, grad_values = attend_backward(
        query, keys, values, segments, attended, logsum, grad_attended
    )
    grad_projected = jnp.concatenate([grad_query, grad_keys, grad_values], axis=1).astype(low)
    grad_projected, ff_all = lax.optimization_barrier((grad_projected, ff_all))
    out_grad = ff_all[:, :out_rows].reshape(-1, D)
    fc_grad = ff_all[:, out_rows:].reshape(-1, FF)
    grad_cols = exchange(grad_projected, "shard", 1, 0)
    grad_normed_first = jnp.dot(grad_projected, qkv_full.T, preferred_element_type=jnp.float32)
    out_later, grad_cols = lax.optimization_barrier((out_part, grad_cols))
    out_sum = lax.psum_scatter(out_later, "shard", scatter_dimension=0, tiled=True)
    result = (residual + out_sum.astype(jnp.float32) + out_bias_full).astype(low)
    term_qkv_weight = jnp.dot(first_all.T, grad_cols, preferred_element_type=jnp.float32) * factor
    term_proj_weight = (
        jnp.dot(attended_cols.T, grad_residual_all, preferred_element_type=jnp.float32) * factor
    )
    attn_terms = jnp.concatenate(
        [
            term_proj_weight.astype(low).reshape(reps, -1, D),
            by_replica(term_qkv_weight.astype(low), shards, reps).reshape(reps, -1, D),
        ],
        axis=1,
    )
    attn_sum = jnp.sum(exchange(attn_terms, "rep", 0, 0).astype(jnp.float32), axis=0).astype(low)
    proj_rows = proj_weight.shape[0] // reps
    proj_piece = attn_sum[:proj_rows]
    qkv_piece = attn_sum[proj_rows:].reshape(D // reps, -1)
    qkv_piece = exchange(qkv_piece, "shard", 0, 1)
    attn_all = spread(jnp.concatenate([proj_piece, qkv_piece.reshape(-1, D)]), "rep").astype(
        jnp.float32
    )
    proj_grad = attn_all[:, :proj_rows].reshape(-1, D)
    qkv_grad = attn_all[:, proj_rows:].reshape(-1, 3 * D)
    grad_input_norm, first_gain_sum, first_shift_sum = first_back(grad_normed_first)
    grad_inputs = grad_residual + grad_input_norm
    terms = jnp.stack(
        [
            first_gain_sum,
            first_shift_sum,
            jnp.sum(grad_query, axis=0),
            jnp.sum(grad_values, axis=0),
            jnp.sum(grad_residual, axis=0),
            second_gain_sum,
            second_shift_sum,
            jnp.sum(cot_f, axis=0),
        ]
    )
    count = terms.shape[0]
    terms = terms.reshape(count, shards, -1).swapaxes(0, 1).reshape(shards, -1)
    own_terms = jnp.concatenate(
        [jnp.sum(exchange(terms, "shard", 0, 0), axis=0), jnp.sum(grad_pre, axis=0)]
    )
    sums = jnp.sum(spread(own_terms, "rep"), axis=0) * factor
    own_cols = D // shards
    fc_bias_grad = sums[count * own_cols :]
    sums = sums[: count * own_cols].reshape(count, own_cols)
    return (
        result,
        grad_inputs,
        sums[0],
        sums[1],
        qkv_grad,
        sums[2:4],
        proj_grad,
        sums[4],
        sums[5],
        sums[6],
        fc_grad,
        fc_bias_grad,
        out_grad,
        sums[7],
    )


def solution(mesh):
    return jax.shard_map(
        per_device,
        mesh=mesh,
        in_specs=(
            P(("rep", "shard"), None),
            P(("rep", "shard"), None),
            P("shard"),
            P("shard"),
            P("shard", None),
            P(None, "shard"),
            P("shard", None),
            P("shard"),
            P("shard"),
            P("shard"),
            P("shard", None),
            P("shard"),
            P("shard", None),
            P("shard"),
            P(("rep", "shard"), None),
        ),
        out_specs=(
            P(("rep", "shard"), None),
            P(("rep", "shard"), None),
            P("shard"),
            P("shard"),
            P("shard", None),
            P(None, "shard"),
            P("shard", None),
            P("shard"),
            P("shard"),
            P("shard"),
            P("shard", None),
            P("shard"),
            P("shard", None),
            P("shard"),
        ),
        check_vma=False,
    )
```

profile of v0, /device:TPU:0, one launch (start us, length us, event | category | flops | bytes accessed | tf_op | source)
XLA Modules:
  0.0 345.6 jit_solution(11735301634824392414)
XLA Ops:
  8.7 1.0 convert_reduce_fusion.1
  9.8 1.1 fusion.28
  11.7 14.5 %all-gather = bf16[8,96,8]{1,2,0:T(8,128)(2,1)S(1)} all-gather(bf16[1,96,8]{1,2,0:T(8,128)(2,1)S(1)} %bitcast.133), channel_id=1, replica_groups=mesh['rep'=4,'shard'=8] {'shard'}, dimensions={0}, use_global_device_ids=true | all-gather | bytes 13824 | tf_op jit(solution)/shard_map/all_gather | solution.py:126
  27.8 1.1 fusion.25
  28.9 25.1 %all-gather.8.cloned.1.call-done = bf16[768,2304]{1,0:T(8,128)(2,1)} async-done(((bf16[96,2304]{1,0:T(8,128)(2,1)}), bf16[768,2304]{1,0:T(8,128)(2,1)}) %all-gather.8.cloned.1.call-update) | async-done | bytes 3538960 | tf_op jit(solution)/shard_map/all_gather | solution.py:130
  53.9 2.6 fusion.57
  58.0 19.2 %all-gather.10.cloned.1.call-done = bf16[768,768]{1,0:T(8,128)(2,1)} async-done(((bf16[96,768]{1,0:T(8,128)(2,1)}), bf16[768,768]{1,0:T(8,128)(2,1)}) %all-gather.10.cloned.1.call-update) | async-done | bytes 1179664 | tf_op jit(solution)/shard_map/all_gather | solution.py:131
  77.2 1.8 fusion.56
  80.6 24.9 %all-gather.12.cloned.1.call-done = bf16[1024,768]{1,0:T(8,128)(2,1)} async-done(((bf16[128,768]{1,0:T(8,128)(2,1)}), bf16[1024,768]{1,0:T(8,128)(2,1)}) %all-gather.12.cloned.1.call-update) | async-done | bytes 1572880 | tf_op jit(solution)/shard_map/all_gather | solution.py:146
  106.4 3.5 %all-to-all-start = ((bf16[96,8,384]{2,0,1:T(8,128)(2,1)}), bf16[96,8,384]{2,0,1:T(8,128)(2,1)S(1)}, u32[]{:S(2)}, u32[]{:S(2)}) async-start(bf16[96,8,384]{2,0,1:T(8,128)(2,1)} %bitcast.106), calls=%async_computation | async-start | bytes 1179648 | tf_op jit(solution)/shard_map/all_to_all | solution.py:78
  110.0 30.8 %all-gather.14.cloned.1.call-done = bf16[1024,768]{1,0:T(8,128)(2,1)} async-done(((bf16[128,768]{1,0:T(8,128)(2,1)}), bf16[1024,768]{1,0:T(8,128)(2,1)}) %all-gather.14.cloned.1.call-update) | async-done | bytes 1572880 | tf_op jit(solution)/shard_map/all_gather | solution.py:148
  140.8 3.6 %fusion.58 = f32[1024,384]{1,0:T(8,128)} fusion(bf16[1024,768]{1,0:T(8,128)(2,1)} %all-gather.14.cloned.1.call-done, bf16[384,768]{1,0:T(8,128)(2,1)S(1)} %copy-done), kind=kOutput, calls=%fused_computation.119 | convolution fusion | flops 603979776 | bytes 3735552 | tf_op jit(solution)/shard_map/dot_general | solution.py:154
  144.4 5.6 %fusion.47 = (f32[384]{0:T(512)}, bf16[1024,384]{1,0:T(8,128)(2,1)S(1)}, f32[1024,384]{1,0:T(8,128)}) fusion(f32[1024,384]{1,0:T(8,128)} %fusion.58, f32[384]{0:T(512)S(1)} %convert_element_type.103, bf16[1024,768]{1,0:T(8,128)(2,1)} %all-gather.12.cloned.1.call-done, bf16[768,384]{1,0:T(8,128)(2,1)S(1)} %bitcast.125), kind=kOutput, calls=%fused_computation.109 | convolution fusion | flops 612630144 | bytes 6097920 | tf_op jit(solution)/shard_map/dot_general | solution.py:149
  150.9 2.2 convolution_convert_fusion
  153.1 2.6 fusion.7
  156.0 2.8 fusion.6
  158.9 19.4 %all_to_all.125 = bf16[4,192,768]{2,1,0:T(8,128)(2,1)S(1)} all-to-all(bf16[4,192,768]{2,1,0:T(8,128)(2,1)S(1)} %pad_maximum_fusion), channel_id=1, replica_groups=mesh['rep'=4,'shard'=8] {'rep'}, dimensions={0} | all-to-all | bytes 2359296 | tf_op jit(solution)/shard_map/all_to_all | solution.py:78
  178.3 0.9 reduce_sum.241
  179.2 7.8 %reduce-scatter.3.cloned.1.call-done = bf16[128,768]{1,0:T(8,128)(2,1)} async-done(((bf16[1024,768]{1,0:T(8,128)(2,1)}), bf16[128,768]{1,0:T(8,128)(2,1)}) %reduce-scatter.3.cloned.1.call-update) | async-done | bytes 196624 | tf_op jit(solution)/shard_map/reduce_scatter | solution.py:160
  187.1 1.7 fusion.53
  188.8 1.7 all_to_all.93
  190.5 4.0 %all-to-all-start.2 = ((bf16[8,24,384]{2,1,0:T(8,128)(2,1)}), bf16[8,24,384]{2,1,0:T(8,128)(2,1)}, u32[]{:S(2)}, u32[]{:S(2)}) async-start(bf16[8,24,384]{2,1,0:T(8,128)(2,1)} %all_to_all.93), calls=%async_computation.3 | async-start | bytes 294912 | tf_op jit(solution)/shard_map/all_to_all | solution.py:78
  194.6 1.8 fusion.30
  197.1 1.2 fusion.49
  199.8 2.1 convolution_convert_fusion.3
  202.0 1.1 copy.140
  203.6 1.9 all-to-all-done.2
  205.4 0.9 copy.145
  206.5 1.1 broadcast_in_dim.34
  207.6 4.6 %all-to-all-start.3 = ((bf16[4,192,768]{2,1,0:T(8,128)(2,1)}), bf16[4,192,768]{2,1,0:T(8,128)(2,1)}, u32[]{:S(2)}, u32[]{:S(2)}) async-start(bf16[4,192,768]{2,1,0:T(8,128)(2,1)} %broadcast_in_dim.34), calls=%async_computation.4 | async-start | bytes 2359296 | tf_op jit(solution)/shard_map/all_to_all | solution.py:78
  213.5 1.1 fusion.51
  215.4 11.7 %all-to-all-done.3 = bf16[4,192,768]{2,1,0:T(8,128)(2,1)} async-done(((bf16[4,192,768]{2,1,0:T(8,128)(2,1)}), bf16[4,192,768]{2,1,0:T(8,128)(2,1)}, u32[]{:S(2)}, u32[]{:S(2)}) %all-to-all-start.3) | async-done | bytes 1179680 | tf_op jit(solution)/shard_map/all_to_all | solution.py:78
  227.1 1.5 convert_element_type.115
  228.6 4.2 %all-to-all-start.4 = ((bf16[128,8,288]{0,2,1:T(8,128)(2,1)}), bf16[128,8,288]{0,2,1:T(8,128)(2,1)}, u32[]{:S(2)}, u32[]{:S(2)}) async-start(bf16[128,8,288]{0,2,1:T(8,128)(2,1)} %bitcast.107), calls=%async_computation.5 | async-start | bytes 1179648 | tf_op jit(solution)/shard_map/all_to_all | solution.py:78
  232.8 3.8 %convolution_convert_fusion.1 = bf16[1024,768]{1,0:T(8,128)(2,1)} fusion(bf16[384,768]{1,0:T(8,128)(2,1)S(1)} %copy-done, f32[1024,384]{1,0:T(8,128)} %get-tuple-element.76), kind=kOutput, calls=%fused_computation.3 | convolution fusion | flops 608305152 | bytes 3735552 | tf_op jit(solution)/shard_map/dot_general | solution.py:165
  236.6 1.3 stack.61
  238.7 1.4 stack.59
  240.7 12.3 %all-to-all-done.4 = bf16[128,8,288]{0,2,1:T(8,128)(2,1)} async-done(((bf16[128,8,288]{0,2,1:T(8,128)(2,1)}), bf16[128,8,288]{0,2,1:T(8,128)(2,1)}, u32[]{:S(2)}, u32[]{:S(2)}) %all-to-all-start.4) | async-done | bytes 589856 | tf_op jit(solution)/shard_map/all_to_all | solution.py:78
  253.0 4.2 %all-to-all-start.7 = ((bf16[128,8,96]{0,2,1:T(8,128)(2,1)}), bf16[128,8,96]{0,2,1:T(8,128)(2,1)}, u32[]{:S(2)}, u32[]{:S(2)}) async-start(bf16[128,8,96]{0,2,1:T(8,128)(2,1)} %bitcast.109), calls=%async_computation.9 | async-start | bytes 393216 | tf_op jit(solution)/shard_map/all_to_all | solution.py:78
  257.2 2.0 copy_bitcast_fusion
  259.3 4.2 %fusion.46 = (f32[768]{0:T(1024)}, f32[128]{0:T(128)S(1)}, f32[128,768]{1,0:T(8,128)S(1)}) fusion(f32[768]{0:T(1024)S(1)} %get-tuple-element.50, f32[128]{0:T(128)S(1)} %copy-done.20, bf16[128,768]{1,0:T(8,128)(2,1)S(1)} %copy-done.1, bf16[128,2304]{0,1:T(8,128)(2,1)} %pad_maximum_fusion.1, bf16[768,2304]{1,0:T(8,128)(2,1)} %all-gather.8.cloned.1.call-done), kind=kOutput, calls=%fused_computation.108 | convolution fusion | flops 453573760 | bytes 4725760 | tf_op jit(solution)/shard_map/dot_general | solution.py:202
  263.8 1.0 convert_reduce_fusion.2
  267.3 3.0 fusion.11
  270.3 2.1 copy.150
  272.4 1.9 copy.151
  274.4 2.8 reshape_reshape.7
  277.1 5.0 %all-to-all-start.5 = ((f32[8,1,768]{2,1,0:T(1,128)}), f32[8,1,768]{2,1,0:T(1,128)S(1)}, u32[]{:S(2)}, u32[]{:S(2)}) async-start(f32[8,1,768]{2,1,0:T(1,128)} %all_to_all.113), calls=%async_computation.7 | async-start | bytes 49152 | tf_op jit(solution)/shard_map/all_to_all | solution.py:78
  282.1 2.0 fusion.14
  285.0 3.0 all-to-all-done.5
  288.0 4.2 %all-to-all-start.8 = ((bf16[4,96,768]{2,1,0:T(8,128)(2,1)}), bf16[4,96,768]{2,1,0:T(8,128)(2,1)}, u32[]{:S(2)}, u32[]{:S(2)}) async-start(bf16[4,96,768]{2,1,0:T(8,128)(2,1)} %pad_maximum_fusion.2), calls=%async_computation.10 | async-start | bytes 1179648 | tf_op jit(solution)/shard_map/all_to_all | solution.py:78
  292.3 9.2 %all-to-all-done.8 = bf16[4,96,768]{2,1,0:T(8,128)(2,1)} async-done(((bf16[4,96,768]{2,1,0:T(8,128)(2,1)}), bf16[4,96,768]{2,1,0:T(8,128)(2,1)}, u32[]{:S(2)}, u32[]{:S(2)}) %all-to-all-start.8) | async-done | bytes 589856 | tf_op jit(solution)/shard_map/all_to_all | solution.py:78
  302.1 3.3 all-to-all-start.6
  305.3 1.2 reduce_sum.257
  307.1 1.8 all_to_all.109
  308.9 1.1 all-to-all-done.6
  310.0 4.0 %all-to-all-start.9 = ((bf16[8,24,288]{2,1,0:T(8,128)(2,1)}), bf16[8,24,288]{2,1,0:T(8,128)(2,1)}, u32[]{:S(2)}, u32[]{:S(2)}) async-start(bf16[8,24,288]{2,1,0:T(8,128)(2,1)} %all_to_all.109), calls=%async_computation.11 | async-start | bytes 294912 | tf_op jit(solution)/shard_map/all_to_all | solution.py:78
  314.0 1.7 fusion.50
  315.7 2.5 reshape.296
  318.3 2.8 all-to-all-done.9
  321.0 0.9 copy.152
  323.1 3.5 %all-to-all-start.10 = ((bf16[4,96,768]{2,1,0:T(8,128)(2,1)}), bf16[4,96,768]{2,1,0:T(8,128)(2,1)S(1)}, u32[]{:S(2)}, u32[]{:S(2)}) async-start(bf16[4,96,768]{2,1,0:T(8,128)(2,1)} %broadcast_in_dim.68), calls=%async_computation.12 | async-start | bytes 1179648 | tf_op jit(solution)/shard_map/all_to_all | solution.py:78
  328.5 6.6 %all-to-all-done.10 = bf16[4,96,768]{2,1,0:T(8,128)(2,1)S(1)} async-done(((bf16[4,96,768]{2,1,0:T(8,128)(2,1)}), bf16[4,96,768]{2,1,0:T(8,128)(2,1)S(1)}, u32[]{:S(2)}, u32[]{:S(2)}) %all-to-all-start.10) | async-done | bytes 589856 | tf_op jit(solution)/shard_map/all_to_all | solution.py:78
  335.2 1.2 reshape.294
  337.1 1.7 add_convert_fusion
  (152 shorter events, 24.1 us)
Async XLA Ops:
  7.2 133.6 %copy-start = (bf16[384,768]{1,0:T(8,128)(2,1)S(1)}, bf16[384,768]{1,0:T(8,128)(2,1)}, u32[]{:S(2)}) copy-start(bf16[384,768]{1,0:T(8,128)(2,1)} %param.27) | copy-start | bytes 1769476
  7.2 46.7 %all-gather.8.cloned.1.call-start = ((), (), s32[]{:S(2)}) async-start(), calls=%async_computation.13 | async-start | bytes 3981312 | tf_op jit(solution)/shard_map/all_gather | solution.py:130
  7.9 69.2 %all-gather.10.cloned.1.call-start = ((), (), s32[]{:S(2)}) async-start(), calls=%async_computation.14 | async-start | bytes 1327104 | tf_op jit(solution)/shard_map/all_gather | solution.py:131
  8.7 96.8 %all-gather.12.cloned.1.call-start = ((), (), s32[]{:S(2)}) async-start(), calls=%async_computation.15 | async-start | bytes 1769472 | tf_op jit(solution)/shard_map/all_gather | solution.py:146
  9.8 46.8 %copy-start.19 = (f32[128]{0:T(128)}, f32[128]{0:T(128)S(1)}, u32[]{:S(2)}) copy-start(f32[128]{0:T(128)S(1)} %broadcast_multiply_fusion.2) | copy-start | bytes 1540
  10.9 0.8 copy-start.30
  10.9 45.7 %copy-start.23 = (f32[128]{0:T(128)}, f32[128]{0:T(128)S(1)}, u32[]{:S(2)}) copy-start(f32[128]{0:T(128)S(1)} %fusion.41) | copy-start | bytes 1540
  28.9 27.7 %copy-start.6 = (bf16[128,768]{1,0:T(8,128)(2,1)}, bf16[128,768]{1,0:T(8,128)(2,1)S(1)}, u32[]{:S(2)}) copy-start(bf16[128,768]{1,0:T(8,128)(2,1)S(1)} %fusion.25) | copy-start | bytes 589828
  56.9 1.1 copy-start.9
  57.1 0.9 copy-start.7
  57.2 19.9 %copy-start.1 = (bf16[128,768]{1,0:T(8,128)(2,1)S(1)}, bf16[128,768]{1,0:T(8,128)(2,1)}, u32[]{:S(2)}) copy-start(bf16[128,768]{1,0:T(8,128)(2,1)} %param.15) | copy-start | bytes 589828
  58.0 145.1 %copy-start.5 = (bf16[12,64,128]{2,1,0:T(8,128)(2,1)}, bf16[12,64,128]{2,1,0:T(8,128)(2,1)S(1)}, u32[]{:S(2)}) copy-start(bf16[12,64,128]{2,1,0:T(8,128)(2,1)S(1)} %convolution_convert_fusion.4) | copy-start | bytes 589828
  77.2 28.4 %copy-start.14 = (bf16[96,3072]{1,0:T(8,128)(2,1)S(1)}, bf16[96,3072]{1,0:T(8,128)(2,1)}, u32[]{:S(2)}) copy-start(bf16[96,3072]{1,0:T(8,128)(2,1)} %param.25) | copy-start | bytes 1769476
  78.9 27.5 %copy-start.22 = (f32[128]{0:T(128)}, f32[128]{0:T(128)S(1)}, u32[]{:S(2)}) copy-start(f32[128]{0:T(128)S(1)} %broadcast_multiply_fusion.1) | copy-start | bytes 1540
  79.1 0.5 copy-start.32
  79.2 27.2 %copy-start.25 = (f32[128]{0:T(128)}, f32[128]{0:T(128)S(1)}, u32[]{:S(2)}) copy-start(f32[128]{0:T(128)S(1)} %fusion.42) | copy-start | bytes 1540
  79.7 30.3 %copy-start.29 = (bf16[384]{0:T(512)(128)(2,1)S(1)}, bf16[384]{0:T(512)(128)(2,1)}, u32[]{:S(2)}) copy-start(bf16[384]{0:T(512)(128)(2,1)} %param.26) | copy-start | bytes 2308
  80.5 60.3 %all-gather.14.cloned.1.call-start = ((), (), s32[]{:S(2)}) async-start(), calls=%async_computation.16 | async-start | bytes 1769472 | tf_op jit(solution)/shard_map/all_gather | solution.py:148
  106.4 38.0 %all-to-all-start = ((bf16[96,8,384]{2,0,1:T(8,128)(2,1)}), bf16[96,8,384]{2,0,1:T(8,128)(2,1)S(1)}, u32[]{:S(2)}, u32[]{:S(2)}) async-start(bf16[96,8,384]{2,0,1:T(8,128)(2,1)} %bitcast.106), calls=%async_computation | async-start | bytes 1179648 | tf_op jit(solution)/shard_map/all_to_all | solution.py:78
  110.0 77.1 %reduce-scatter.3.cloned.1.call-start = ((), (), s32[]{:S(2)}) async-start(), calls=%async_computation.17 | async-start | bytes 1769472 | tf_op jit(solution)/shard_map/reduce_scatter | solution.py:160
  150.0 0.9 copy-start.33
  153.1 114.3 %all-gather.18.cloned.1.call-start = ((), (), s32[]{:S(2)}) async-start(), calls=%async_computation.20 | async-start | bytes 1769472 | tf_op jit(solution)/shard_map/all_gather | solution.py:177
  188.8 11.0 %copy-start.2 = (bf16[768,768]{1,0:T(8,128)(2,1)S(1)}, bf16[768,768]{1,0:T(8,128)(2,1)}, u32[]{:S(2)}) copy-start(bf16[768,768]{1,0:T(8,128)(2,1)} %all-gather.10.cloned.1.call-done) | copy-start | bytes 3538948
  190.5 14.9 %all-to-all-start.2 = ((bf16[8,24,384]{2,1,0:T(8,128)(2,1)}), bf16[8,24,384]{2,1,0:T(8,128)(2,1)}, u32[]{:S(2)}, u32[]{:S(2)}) async-start(bf16[8,24,384]{2,1,0:T(8,128)(2,1)} %all_to_all.93), calls=%async_computation.3 | async-start | bytes 294912 | tf_op jit(solution)/shard_map/all_to_all | solution.py:78
  194.5 87.6 %all-gather.16.cloned.1.call-start = ((), (), s32[]{:S(2)}) async-start(), calls=%async_computation.19 | async-start | bytes 1769472 | tf_op jit(solution)/shard_map/all_gather | solution.py:182
  194.6 4.4 %copy-start.12 = (bf16[128,768]{1,0:T(8,128)(2,1)S(1)}, bf16[128,768]{1,0:T(8,128)(2,1)}, u32[]{:S(2)}) copy-start(bf16[128,768]{1,0:T(8,128)(2,1)} %param.29) | copy-start | bytes 589828
  198.3 0.8 copy-start.3
  198.3 0.7 copy-start.27
  202.0 4.5 %copy-start.15 = (bf16[96,768]{1,0:T(8,128)(2,1)S(1)}, bf16[96,768]{1,0:T(8,128)(2,1)}, u32[]{:S(2)}) copy-start(bf16[96,768]{1,0:T(8,128)(2,1)} %get-tuple-element.64) | copy-start | bytes 442372
  206.5 5.7 %copy-start.10 = (bf16[128,768]{0,1:T(8,128)(2,1)S(1)}, bf16[128,768]{0,1:T(8,128)(2,1)}, u32[]{:S(2)}) copy-start(bf16[128,768]{0,1:T(8,128)(2,1)} %copy-done.9) | copy-start | bytes 589828
  207.6 5.0 %copy-start.8 = (bf16[128,768]{0,1:T(8,128)(2,1)S(1)}, bf16[128,768]{0,1:T(8,128)(2,1)}, u32[]{:S(2)}) copy-start(bf16[128,768]{0,1:T(8,128)(2,1)} %copy-done.7) | copy-start | bytes 589828
  207.6 19.6 %all-to-all-start.3 = ((bf16[4,192,768]{2,1,0:T(8,128)(2,1)}), bf16[4,192,768]{2,1,0:T(8,128)(2,1)}, u32[]{:S(2)}, u32[]{:S(2)}) async-start(bf16[4,192,768]{2,1,0:T(8,128)(2,1)} %broadcast_in_dim.34), calls=%async_computation.4 | async-start | bytes 2359296 | tf_op jit(solution)/shard_map/all_to_all | solution.py:78
  228.6 24.4 %all-to-all-start.4 = ((bf16[128,8,288]{0,2,1:T(8,128)(2,1)}), bf16[128,8,288]{0,2,1:T(8,128)(2,1)}, u32[]{:S(2)}, u32[]{:S(2)}) async-start(bf16[128,8,288]{0,2,1:T(8,128)(2,1)} %bitcast.107), calls=%async_computation.5 | async-start | bytes 1179648 | tf_op jit(solution)/shard_map/all_to_all | solution.py:78
  232.8 5.2 %copy-start.18 = (f32[768]{0:T(1024)S(1)}, f32[768]{0:T(1024)}, u32[]{:S(2)}) copy-start(f32[768]{0:T(1024)} %get-tuple-element.42) | copy-start | bytes 9220
  232.8 7.2 %copy-start.16 = (f32[12,64]{1,0:T(8,128)S(1)}, f32[12,64]{1,0:T(8,128)}, u32[]{:S(2)}) copy-start(f32[12,64]{1,0:T(8,128)} %get-tuple-element.62) | copy-start | bytes 9220
  253.0 6.2 %copy-start.20 = (f32[128]{0:T(128)S(1)}, f32[128]{0:T(128)}, u32[]{:S(2)}) copy-start(f32[128]{0:T(128)} %copy-done.19) | copy-start | bytes 1540
  253.0 24.1 %all-to-all-start.7 = ((bf16[128,8,96]{0,2,1:T(8,128)(2,1)}), bf16[128,8,96]{0,2,1:T(8,128)(2,1)}, u32[]{:S(2)}, u32[]{:S(2)}) async-start(bf16[128,8,96]{0,2,1:T(8,128)(2,1)} %bitcast.109), calls=%async_computation.9 | async-start | bytes 393216 | tf_op jit(solution)/shard_map/all_to_all | solution.py:78
  257.1 79.9 %reduce-scatter.5.cloned.1.call-start = ((), (), s32[]{:S(2)}) async-start(), calls=%async_computation.18 | async-start | bytes 1769472 | tf_op jit(solution)/shard_map/reduce_scatter | solution.py:204
  259.2 4.3 %copy-start.31 = (f32[128]{0:T(128)S(1)}, f32[128]{0:T(128)}, u32[]{:S(2)}) copy-start(f32[128]{0:T(128)} %copy-done.30) | copy-start | bytes 1540
  259.2 4.3 %copy-start.24 = (f32[128]{0:T(128)S(1)}, f32[128]{0:T(128)}, u32[]{:S(2)}) copy-start(f32[128]{0:T(128)} %copy-done.23) | copy-start | bytes 1540
  259.2 4.6 %copy-start.4 = (f32[128,768]{1,0:T(8,128)S(1)}, f32[128,768]{1,0:T(8,128)}, u32[]{:S(2)}) copy-start(f32[128,768]{1,0:T(8,128)} %copy-done.3) | copy-start | bytes 1179652
  259.2 4.6 %copy-start.13 = (bf16[128,768]{1,0:T(8,128)(2,1)S(1)}, bf16[128,768]{1,0:T(8,128)(2,1)}, u32[]{:S(2)}) copy-start(bf16[128,768]{1,0:T(8,128)(2,1)} %param.29) | copy-start | bytes 589828
  259.2 4.6 %copy-start.21 = (f32[128]{0:T(128)S(1)}, f32[128]{0:T(128)}, u32[]{:S(2)}) copy-start(f32[128]{0:T(128)} %copy-done.19) | copy-start | bytes 1540
  259.2 4.6 %copy-start.28 = (f32[128]{0:T(128)S(1)}, f32[128]{0:T(128)}, u32[]{:S(2)}) copy-start(f32[128]{0:T(128)} %copy-done.27) | copy-start | bytes 1540
  277.1 10.9 %all-to-all-start.5 = ((f32[8,1,768]{2,1,0:T(1,128)}), f32[8,1,768]{2,1,0:T(1,128)S(1)}, u32[]{:S(2)}, u32[]{:S(2)}) async-start(f32[8,1,768]{2,1,0:T(1,128)} %all_to_all.113), calls=%async_computation.7 | async-start | bytes 49152 | tf_op jit(solution)/shard_map/all_to_all | solution.py:78
  282.1 2.0 copy-start.11
  284.1 8.1 %copy-start.26 = (f32[384]{0:T(512)S(1)}, f32[384]{0:T(512)}, u32[]{:S(2)}) copy-start(f32[384]{0:T(512)} %get-tuple-element.51) | copy-start | bytes 4612
  288.0 13.4 %all-to-all-start.8 = ((bf16[4,96,768]{2,1,0:T(8,128)(2,1)}), bf16[4,96,768]{2,1,0:T(8,128)(2,1)}, u32[]{:S(2)}, u32[]{:S(2)}) async-start(bf16[4,96,768]{2,1,0:T(8,128)(2,1)} %pad_maximum_fusion.2), calls=%async_computation.10 | async-start | bytes 1179648 | tf_op jit(solution)/shard_map/all_to_all | solution.py:78
  302.1 7.9 %all-to-all-start.6 = ((f32[4,1,1152]{2,1,0:T(1,128)}), f32[4,1,1152]{2,1,0:T(1,128)S(1)}, u32[]{:S(2)}, u32[]{:S(2)}) async-start(f32[4,1,1152]{2,1,0:T(1,128)} %broadcast_in_dim.37), calls=%async_computation.8 | async-start | bytes 36864 | tf_op jit(solution)/shard_map/all_to_all | solution.py:78
  310.0 11.0 %all-to-all-start.9 = ((bf16[8,24,288]{2,1,0:T(8,128)(2,1)}), bf16[8,24,288]{2,1,0:T(8,128)(2,1)}, u32[]{:S(2)}, u32[]{:S(2)}) async-start(bf16[8,24,288]{2,1,0:T(8,128)(2,1)} %all_to_all.109), calls=%async_computation.11 | async-start | bytes 294912 | tf_op jit(solution)/shard_map/all_to_all | solution.py:78
  323.1 12.0 %all-to-all-start.10 = ((bf16[4,96,768]{2,1,0:T(8,128)(2,1)}), bf16[4,96,768]{2,1,0:T(8,128)(2,1)S(1)}, u32[]{:S(2)}, u32[]{:S(2)}) async-start(bf16[4,96,768]{2,1,0:T(8,128)(2,1)} %broadcast_in_dim.68), calls=%async_computation.12 | async-start | bytes 1179648 | tf_op jit(solution)/shard_map/all_to_all | solution.py:78
  335.2 1.9 copy-start.17
Sparse Core Ops, SparseCore 0:
  9.7 44.2 all-gather.7
  55.6 21.5 all-gather.9
  80.6 24.8 all-gather.11
  107.0 33.7 all-gather.13
  153.2 33.8 reduce-scatter.2
  188.6 26.5 all-gather.17
  217.4 27.5 all-gather.15
  260.3 35.7 reduce-scatter.4
where the time goes:
time: 347 us; the launch traced here: 346 us
  waiting for transfers between devices  158 us (46%)
  starting transfers between devices  40.7 us (12%)
  local copies, waits for them, and re-layouts  40.4 us (12%)
  matrix products  39.6 us (11%)
  blocking collectives  33.9 us (10%)
  other arithmetic  18.2 us (5%)
  between operations  14.9 us (4%)
    all_to_all x10, waiting for transfers between devices, exchange(): lax.all_to_all(field, axis, split_axis=split, concat_axis=concat, tiled=T...  48.6 us
    all_to_all x10, starting transfers between devices, exchange(): lax.all_to_all(field, axis, split_axis=split, concat_axis=concat, tiled=T...  40.4 us
    all_gather x1, waiting for transfers between devices, per_device(): cot_all = lax.all_gather(cot_later, 'shard', axis=0, tiled=True)  30.8 us
    all_gather x1, waiting for transfers between devices, per_device(): qkv_full = lax.all_gather(qkv_weight, 'shard', axis=0, tiled=True)  25.1 us
    all_gather x1, waiting for transfers between devices, per_device(): lax.all_gather(normed_s.astype(low), 'shard', axis=0, tiled=True)  24.9 us
    all_to_all x1, blocking collectives, exchange(): lax.all_to_all(field, axis, split_axis=split, concat_axis=concat, tiled=T...  19.4 us
    all_gather x1, waiting for transfers between devices, per_device(): proj_full = lax.all_gather(proj_weight, 'shard', axis=0, tiled=True)  19.2 us
    all_gather x1, blocking collectives, per_device(): lax.all_gather(small, 'shard', axis=1, tiled=True).astype(jnp.float32)  14.5 us
  transfers between devices with their start and end apart: 18, of which 13 were waited for; matrix products, arithmetic and copies ran while one was open for 23% of the time, Pallas kernels for 0%

commit v1 on v0

--- a/solution.py
+++ b/solution.py
@@ -127,8 +127,13 @@
     gain_one, shift_one, q_bias, v_bias, proj_bias_full, gain_two, shift_two, out_bias_full = (
         small_full[i] for i in range(8)
     )
-    qkv_full = lax.all_gather(qkv_weight, "shard", axis=0, tiled=True)
-    proj_full = lax.all_gather(proj_weight, "shard", axis=0, tiled=True)
+    qkv_full, proj_full = jnp.split(
+        lax.all_gather(
+            jnp.concatenate([qkv_weight, proj_weight], axis=1), "shard", axis=0, tiled=True
+        ),
+        [qkv_weight.shape[1]],
+        axis=1,
+    )
     fc_cols = exchange(fc_weight, "shard", 1, 0)
     inputs = tokens.astype(jnp.float32)
     normed_f, first_back = jax.vjp(layer_norm, inputs, gain_one, shift_one)

time: 347 us -> 336 us (0.968)
  waiting for transfers between devices: 158 us -> 153 us
  local copies, waits for them, and re-layouts: 40.4 us -> 36.2 us
    all_gather x2 -> x1, waiting for transfers between devices: 44.2 us -> 39.4 us  [per_device(): lax.all_gather(jnp.concatenate([qkv_weight, proj_weight], axis=1), 'shard...]
  transfers between devices with their start and end apart: 18 -> 17, of which waited for: 13 -> 12; matrix products, arithmetic and copies ran while one was open for 23% -> 20% of each run, Pallas kernels for 0% -> 0%
where the time goes in v1:
time: 336 us; the launch traced here: 334 us
  waiting for transfers between devices  153 us (46%)
  starting transfers between devices  41.7 us (12%)
  matrix products  39.5 us (12%)
  local copies, waits for them, and re-layouts  36.2 us (11%)
  blocking collectives  33.8 us (10%)
  other arithmetic  15.2 us (5%)
  between operations  15 us (4%)
    all_to_all x10, waiting for transfers between devices, exchange(): lax.all_to_all(field, axis, split_axis=split, concat_axis=concat, tiled=T...  51.2 us
    all_to_all x10, starting transfers between devices, exchange(): lax.all_to_all(field, axis, split_axis=split, concat_axis=concat, tiled=T...  41.4 us
    all_gather x1, waiting for transfers between devices, per_device(): lax.all_gather(jnp.concatenate([qkv_weight, proj_weight], axis=1), 'shard...  39.4 us
    all_gather x1, waiting for transfers between devices, per_device(): cot_all = lax.all_gather(cot_later, 'shard', axis=0, tiled=True)  30.8 us
    all_gather x1, waiting for transfers between devices, per_device(): lax.all_gather(normed_s.astype(low), 'shard', axis=0, tiled=True)  24 us
    all_to_all x1, blocking collectives, exchange(): lax.all_to_all(field, axis, split_axis=split, concat_axis=concat, tiled=T...  19.4 us
    all_gather x1, blocking collectives, per_device(): lax.all_gather(small, 'shard', axis=1, tiled=True).astype(jnp.float32)  14.4 us
    reduce_scatter x1, waiting for transfers between devices, per_device(): lax.psum_scatter(grad_normed_part, 'shard', scatter_dimension=0, tiled=True)  7.55 us
  transfers between devices with their start and end apart: 17, of which 12 were waited for; matrix products, arithmetic and copies ran while one was open for 20% of the time, Pallas kernels for 0%

profile of v1, /device:TPU:0, one launch (start us, length us, event | category | flops | bytes accessed | tf_op | source)
XLA Modules:
  0.0 334.4 jit_solution(2015553096293627685)
XLA Ops:
  7.3 2.1 pad_maximum_fusion.1
  9.6 14.4 %all-gather = bf16[8,96,8]{1,2,0:T(8,128)(2,1)S(1)} all-gather(bf16[1,96,8]{1,2,0:T(8,128)(2,1)S(1)} %bitcast.130), channel_id=1, replica_groups=mesh['rep'=4,'shard'=8] {'shard'}, dimensions={0}, use_global_device_ids=true | all-gather | bytes 13824 | tf_op jit(solution)/shard_map/all_gather | solution.py:126
  25.3 39.4 %all-gather.7.cloned.1.call-done = bf16[768,3072]{1,0:T(8,128)(2,1)} async-done(((bf16[96,3072]{1,0:T(8,128)(2,1)}), bf16[768,3072]{1,0:T(8,128)(2,1)}) %all-gather.7.cloned.1.call-update) | async-done | bytes 4718608 | tf_op jit(solution)/shard_map/all_gather | solution.py:131
  64.8 2.6 fusion.2
  68.8 1.8 fusion.62
  71.4 0.8 add_convert_fusion.1
  72.3 24.0 %all-gather.9.cloned.1.call-done = bf16[1024,768]{1,0:T(8,128)(2,1)} async-done(((bf16[128,768]{1,0:T(8,128)(2,1)}), bf16[1024,768]{1,0:T(8,128)(2,1)}) %all-gather.9.cloned.1.call-update) | async-done | bytes 1572880 | tf_op jit(solution)/shard_map/all_gather | solution.py:151
  96.3 0.9 copy.177
  97.2 3.5 %all-to-all-start = ((bf16[96,8,384]{2,0,1:T(8,128)(2,1)}), bf16[96,8,384]{2,0,1:T(8,128)(2,1)S(1)}, u32[]{:S(2)}, u32[]{:S(2)}) async-start(bf16[96,8,384]{2,0,1:T(8,128)(2,1)} %bitcast.102), calls=%async_computation | async-start | bytes 1179648 | tf_op jit(solution)/shard_map/all_to_all | solution.py:78
  100.8 30.8 %all-gather.11.cloned.1.call-done = bf16[1024,768]{1,0:T(8,128)(2,1)} async-done(((bf16[128,768]{1,0:T(8,128)(2,1)}), bf16[1024,768]{1,0:T(8,128)(2,1)}) %all-gather.11.cloned.1.call-update) | async-done | bytes 1572880 | tf_op jit(solution)/shard_map/all_gather | solution.py:153
  131.6 3.6 %fusion.63 = f32[1024,384]{1,0:T(8,128)} fusion(bf16[1024,768]{1,0:T(8,128)(2,1)} %all-gather.11.cloned.1.call-done, bf16[384,768]{1,0:T(8,128)(2,1)S(1)} %copy-done), kind=kOutput, calls=%fused_computation.125 | convolution fusion | flops 603979776 | bytes 3735552 | tf_op jit(solution)/shard_map/dot_general | solution.py:159
  135.1 5.5 %fusion.53 = (f32[384]{0:T(512)}, bf16[1024,384]{1,0:T(8,128)(2,1)S(1)}, f32[1024,384]{1,0:T(8,128)}) fusion(f32[1024,384]{1,0:T(8,128)} %fusion.63, f32[384]{0:T(512)S(1)} %convert_element_type.103, bf16[1024,768]{1,0:T(8,128)(2,1)} %all-gather.9.cloned.1.call-done, bf16[768,384]{1,0:T(8,128)(2,1)S(1)} %bitcast.121), kind=kOutput, calls=%fused_computation.116 | convolution fusion | flops 612630144 | bytes 6097920 | tf_op jit(solution)/shard_map/dot_general | solution.py:154
  140.7 0.9 copy-done.43
  141.6 2.2 convolution_convert_fusion
  143.9 2.6 fusion.11
  146.8 2.8 fusion.10
  149.7 19.4 %all_to_all.125 = bf16[4,192,768]{2,1,0:T(8,128)(2,1)S(1)} all-to-all(bf16[4,192,768]{2,1,0:T(8,128)(2,1)S(1)} %pad_maximum_fusion), channel_id=1, replica_groups=mesh['rep'=4,'shard'=8] {'rep'}, dimensions={0} | all-to-all | bytes 2359296 | tf_op jit(solution)/shard_map/all_to_all | solution.py:78
  169.1 0.9 reduce_sum.241
  170.0 7.5 %reduce-scatter.3.cloned.1.call-done = bf16[128,768]{1,0:T(8,128)(2,1)} async-done(((bf16[1024,768]{1,0:T(8,128)(2,1)}), bf16[128,768]{1,0:T(8,128)(2,1)}) %reduce-scatter.3.cloned.1.call-update) | async-done | bytes 196624 | tf_op jit(solution)/shard_map/reduce_scatter | solution.py:165
  177.6 1.0 fusion.59
  179.4 3.4 %all-to-all-start.2 = ((bf16[8,24,384]{2,1,0:T(8,128)(2,1)}), bf16[8,24,384]{2,1,0:T(8,128)(2,1)S(1)}, u32[]{:S(2)}, u32[]{:S(2)}) async-start(bf16[8,24,384]{2,1,0:T(8,128)(2,1)} %all_to_all.93), calls=%async_computation.3 | async-start | bytes 294912 | tf_op jit(solution)/shard_map/all_to_all | solution.py:78
  182.8 1.8 fusion.36
  186.4 1.9 convolution_convert_fusion.3
  189.0 1.6 all-to-all-done.2
  190.7 1.1 broadcast_in_dim.34
  191.8 5.1 %all-to-all-start.3 = ((bf16[4,192,768]{2,1,0:T(8,128)(2,1)}), bf16[4,192,768]{2,1,0:T(8,128)(2,1)}, u32[]{:S(2)}, u32[]{:S(2)}) async-start(bf16[4,192,768]{2,1,0:T(8,128)(2,1)} %broadcast_in_dim.34), calls=%async_computation.4 | async-start | bytes 2359296 | tf_op jit(solution)/shard_map/all_to_all | solution.py:78
  197.3 0.9 fusion.58
  198.2 1.1 fusion.57
  199.2 0.9 pad_maximum_fusion.2
  200.1 10.5 %all-to-all-done.3 = bf16[4,192,768]{2,1,0:T(8,128)(2,1)} async-done(((bf16[4,192,768]{2,1,0:T(8,128)(2,1)}), bf16[4,192,768]{2,1,0:T(8,128)(2,1)}, u32[]{:S(2)}, u32[]{:S(2)}) %all-to-all-start.3) | async-done | bytes 1179680 | tf_op jit(solution)/shard_map/all_to_all | solution.py:78
  210.6 1.5 convert_element_type.115
  212.1 5.4 %all-to-all-start.4 = ((bf16[128,8,288]{0,2,1:T(8,128)(2,1)}), bf16[128,8,288]{0,2,1:T(8,128)(2,1)}, u32[]{:S(2)}, u32[]{:S(2)}) async-start(bf16[128,8,288]{0,2,1:T(8,128)(2,1)} %bitcast.108), calls=%async_computation.5 | async-start | bytes 1179648 | tf_op jit(solution)/shard_map/all_to_all | solution.py:78
  217.5 3.8 %convolution_convert_fusion.1 = bf16[1024,768]{1,0:T(8,128)(2,1)} fusion(bf16[384,768]{1,0:T(8,128)(2,1)S(1)} %copy-done, f32[1024,384]{1,0:T(8,128)} %get-tuple-element.76), kind=kOutput, calls=%fused_computation.7 | convolution fusion | flops 608305152 | bytes 3735552 | tf_op jit(solution)/shard_map/dot_general | solution.py:170
  221.3 1.3 stack.61
  223.3 1.4 stack.59
  225.4 16.4 %all-to-all-done.4 = bf16[128,8,288]{0,2,1:T(8,128)(2,1)} async-done(((bf16[128,8,288]{0,2,1:T(8,128)(2,1)}), bf16[128,8,288]{0,2,1:T(8,128)(2,1)}, u32[]{:S(2)}, u32[]{:S(2)}) %all-to-all-start.4) | async-done | bytes 589856 | tf_op jit(solution)/shard_map/all_to_all | solution.py:78
  241.8 4.1 %all-to-all-start.7 = ((bf16[128,8,96]{0,2,1:T(8,128)(2,1)}), bf16[128,8,96]{0,2,1:T(8,128)(2,1)}, u32[]{:S(2)}, u32[]{:S(2)}) async-start(bf16[128,8,96]{0,2,1:T(8,128)(2,1)} %bitcast.104), calls=%async_computation.9 | async-start | bytes 393216 | tf_op jit(solution)/shard_map/all_to_all | solution.py:78
  246.0 2.0 copy_bitcast_fusion
  248.1 4.2 %fusion.52 = (f32[768]{0:T(1024)}, f32[128]{0:T(128)S(1)}, f32[128,768]{1,0:T(8,128)S(1)}) fusion(f32[768]{0:T(1024)S(1)} %get-tuple-element.50, f32[128]{0:T(128)S(1)} %copy-done.19, bf16[128,768]{1,0:T(8,128)(2,1)S(1)} %copy-done.1, bf16[128,2304]{0,1:T(8,128)(2,1)} %pad_maximum_fusion.2, bf16[768,3072]{1,0:T(8,128)(2,1)} %all-gather.7.cloned.1.call-done), kind=kOutput, calls=%fused_computation.115 | convolution fusion | flops 453573760 | bytes 4725760 | tf_op jit(solution)/shard_map/dot_general | solution.py:207
  252.6 1.0 convert_reduce_fusion.2
  256.2 3.0 fusion.15
  259.2 2.1 copy.150
  261.2 1.9 copy.151
  263.2 2.8 reshape_reshape.7
  265.9 5.0 %all-to-all-start.5 = ((f32[8,1,768]{2,1,0:T(1,128)}), f32[8,1,768]{2,1,0:T(1,128)S(1)}, u32[]{:S(2)}, u32[]{:S(2)}) async-start(f32[8,1,768]{2,1,0:T(1,128)} %all_to_all.113), calls=%async_computation.7 | async-start | bytes 49152 | tf_op jit(solution)/shard_map/all_to_all | solution.py:78
  270.9 2.0 fusion.18
  272.9 0.9 pad_maximum_fusion.3
  273.8 3.1 all-to-all-done.5
  276.9 4.2 %all-to-all-start.8 = ((bf16[4,96,768]{2,1,0:T(8,128)(2,1)}), bf16[4,96,768]{2,1,0:T(8,128)(2,1)}, u32[]{:S(2)}, u32[]{:S(2)}) async-start(bf16[4,96,768]{2,1,0:T(8,128)(2,1)} %pad_maximum_fusion.3), calls=%async_computation.10 | async-start | bytes 1179648 | tf_op jit(solution)/shard_map/all_to_all | solution.py:78
  281.2 9.1 %all-to-all-done.8 = bf16[4,96,768]{2,1,0:T(8,128)(2,1)} async-done(((bf16[4,96,768]{2,1,0:T(8,128)(2,1)}), bf16[4,96,768]{2,1,0:T(8,128)(2,1)}, u32[]{:S(2)}, u32[]{:S(2)}) %all-to-all-start.8) | async-done | bytes 589856 | tf_op jit(solution)/shard_map/all_to_all | solution.py:78
  290.9 3.3 all-to-all-start.6
  294.1 1.2 reduce_sum.257
  295.9 1.8 all_to_all.109
  297.8 1.1 all-to-all-done.6
  298.8 4.0 %all-to-all-start.9 = ((bf16[8,24,288]{2,1,0:T(8,128)(2,1)}), bf16[8,24,288]{2,1,0:T(8,128)(2,1)}, u32[]{:S(2)}, u32[]{:S(2)}) async-start(bf16[8,24,288]{2,1,0:T(8,128)(2,1)} %all_to_all.109), calls=%async_computation.11 | async-start | bytes 294912 | tf_op jit(solution)/shard_map/all_to_all | solution.py:78
  302.8 1.6 fusion.56
  304.5 2.5 reshape.296
  307.0 2.8 all-to-all-done.9
  309.8 0.9 copy.152
  311.0 0.9 broadcast_in_dim.68
  311.9 3.5 %all-to-all-start.10 = ((bf16[4,96,768]{2,1,0:T(8,128)(2,1)}), bf16[4,96,768]{2,1,0:T(8,128)(2,1)S(1)}, u32[]{:S(2)}, u32[]{:S(2)}) async-start(bf16[4,96,768]{2,1,0:T(8,128)(2,1)} %broadcast_in_dim.68), calls=%async_computation.12 | async-start | bytes 1179648 | tf_op jit(solution)/shard_map/all_to_all | solution.py:78
  317.3 6.6 %all-to-all-done.10 = bf16[4,96,768]{2,1,0:T(8,128)(2,1)S(1)} async-done(((bf16[4,96,768]{2,1,0:T(8,128)(2,1)}), bf16[4,96,768]{2,1,0:T(8,128)(2,1)S(1)}, u32[]{:S(2)}, u32[]{:S(2)}) %all-to-all-start.10) | async-done | bytes 589856 | tf_op jit(solution)/shard_map/all_to_all | solution.py:78
  324.0 1.2 reshape.294
  325.9 1.7 add_convert_fusion
  (170 shorter events, 16.1 us)
Async XLA Ops:
  7.2 124.4 %copy-start = (bf16[384,768]{1,0:T(8,128)(2,1)S(1)}, bf16[384,768]{1,0:T(8,128)(2,1)}, u32[]{:S(2)}) copy-start(bf16[384,768]{1,0:T(8,128)(2,1)} %param.27) | copy-start | bytes 1769476
  7.2 2.3 copy-start.42
  7.2 2.3 copy-start.41
  7.2 2.3 copy-start.40
  7.2 2.3 copy-start.39
  7.2 2.3 copy-start.38
  7.2 2.3 copy-start.37
  7.3 2.3 copy-start.36
  7.3 17.4 %copy-start.1 = (bf16[128,768]{1,0:T(8,128)(2,1)S(1)}, bf16[128,768]{1,0:T(8,128)(2,1)}, u32[]{:S(2)}) copy-start(bf16[128,768]{1,0:T(8,128)(2,1)} %param.15) | copy-start | bytes 589828
  7.3 17.8 %copy-start.28 = (s32[1,128]{1,0:T(1,128)S(1)}, s32[1,128]{1,0:T(1,128)}, u32[]{:S(2)}) copy-start(s32[1,128]{1,0:T(1,128)} %param.16) | copy-start | bytes 1540
  7.3 57.5 %all-gather.7.cloned.1.call-start = ((), (), s32[]{:S(2)}) async-start(), calls=%async_computation.13 | async-start | bytes 5308416 | tf_op jit(solution)/shard_map/all_gather | solution.py:131
  9.4 86.8 %all-gather.9.cloned.1.call-start = ((), (), s32[]{:S(2)}) async-start(), calls=%async_computation.14 | async-start | bytes 1769472 | tf_op jit(solution)/shard_map/all_gather | solution.py:151
  24.8 42.6 %copy-start.18 = (f32[128]{0:T(128)}, f32[128]{0:T(128)S(1)}, u32[]{:S(2)}) copy-start(f32[128]{0:T(128)S(1)} %broadcast_multiply_fusion.2) | copy-start | bytes 1540
  25.0 42.4 %copy-start.32 = (f32[128]{0:T(128)}, f32[128]{0:T(128)S(1)}, u32[]{:S(2)}) copy-start(f32[128]{0:T(128)S(1)} %fusion.34) | copy-start | bytes 1540
  25.0 42.4 %copy-start.23 = (f32[128]{0:T(128)}, f32[128]{0:T(128)S(1)}, u32[]{:S(2)}) copy-start(f32[128]{0:T(128)S(1)} %fusion.47) | copy-start | bytes 1540
  25.3 42.1 %copy-start.5 = (bf16[128,768]{1,0:T(8,128)(2,1)}, bf16[128,768]{1,0:T(8,128)(2,1)S(1)}, u32[]{:S(2)}) copy-start(bf16[128,768]{1,0:T(8,128)(2,1)S(1)} %fusion.31) | copy-start | bytes 589828
  67.7 1.1 copy-start.8
  67.9 0.9 copy-start.6
  68.8 119.7 %copy-start.4 = (bf16[12,64,128]{2,1,0:T(8,128)(2,1)}, bf16[12,64,128]{2,1,0:T(8,128)(2,1)S(1)}, u32[]{:S(2)}) copy-start(bf16[12,64,128]{2,1,0:T(8,128)(2,1)S(1)} %convolution_convert_fusion.4) | copy-start | bytes 589828
  68.8 27.4 %copy-start.14 = (bf16[96,3072]{1,0:T(8,128)(2,1)S(1)}, bf16[96,3072]{1,0:T(8,128)(2,1)}, u32[]{:S(2)}) copy-start(bf16[96,3072]{1,0:T(8,128)(2,1)} %param.25) | copy-start | bytes 1769476
  70.7 26.5 %copy-start.21 = (f32[128]{0:T(128)}, f32[128]{0:T(128)S(1)}, u32[]{:S(2)}) copy-start(f32[128]{0:T(128)S(1)} %broadcast_multiply_fusion.1) | copy-start | bytes 1540
  70.9 0.5 copy-start.34
  70.9 26.3 %copy-start.25 = (f32[128]{0:T(128)}, f32[128]{0:T(128)S(1)}, u32[]{:S(2)}) copy-start(f32[128]{0:T(128)S(1)} %fusion.48) | copy-start | bytes 1540
  71.4 29.4 %copy-start.31 = (bf16[384]{0:T(512)(128)(2,1)S(1)}, bf16[384]{0:T(512)(128)(2,1)}, u32[]{:S(2)}) copy-start(bf16[384]{0:T(512)(128)(2,1)} %param.26) | copy-start | bytes 2308
  72.2 59.3 %all-gather.11.cloned.1.call-start = ((), (), s32[]{:S(2)}) async-start(), calls=%async_computation.15 | async-start | bytes 1769472 | tf_op jit(solution)/shard_map/all_gather | solution.py:153
  97.2 38.0 %all-to-all-start = ((bf16[96,8,384]{2,0,1:T(8,128)(2,1)}), bf16[96,8,384]{2,0,1:T(8,128)(2,1)S(1)}, u32[]{:S(2)}, u32[]{:S(2)}) async-start(bf16[96,8,384]{2,0,1:T(8,128)(2,1)} %bitcast.102), calls=%async_computation | async-start | bytes 1179648 | tf_op jit(solution)/shard_map/all_to_all | solution.py:78
  100.7 76.9 %reduce-scatter.3.cloned.1.call-start = ((), (), s32[]{:S(2)}) async-start(), calls=%async_computation.16 | async-start | bytes 1769472 | tf_op jit(solution)/shard_map/reduce_scatter | solution.py:165
  140.7 0.9 copy-start.43
  143.8 112.3 %all-gather.15.cloned.1.call-start = ((), (), s32[]{:S(2)}) async-start(), calls=%async_computation.19 | async-start | bytes 1769472 | tf_op jit(solution)/shard_map/all_gather | solution.py:182
  170.0 14.6 %copy-start.35 = (f32[128]{0:T(128)S(1)}, f32[128]{0:T(128)}, u32[]{:S(2)}) copy-start(f32[128]{0:T(128)} %copy-done.34) | copy-start | bytes 1540
  170.0 14.6 %copy-start.22 = (f32[128]{0:T(128)S(1)}, f32[128]{0:T(128)}, u32[]{:S(2)}) copy-start(f32[128]{0:T(128)} %copy-done.21) | copy-start | bytes 1540
  170.0 14.6 %copy-start.26 = (f32[128]{0:T(128)S(1)}, f32[128]{0:T(128)}, u32[]{:S(2)}) copy-start(f32[128]{0:T(128)} %copy-done.25) | copy-start | bytes 1540
  170.0 15.6 %copy-start.11 = (bf16[128,768]{1,0:T(8,128)(2,1)S(1)}, bf16[128,768]{1,0:T(8,128)(2,1)}, u32[]{:S(2)}) copy-start(bf16[128,768]{1,0:T(8,128)(2,1)} %param.29) | copy-start | bytes 589828
  177.6 7.1 %copy-start.13 = (bf16[128,768]{1,0:T(8,128)(2,1)S(1)}, bf16[128,768]{1,0:T(8,128)(2,1)}, u32[]{:S(2)}) copy-start(bf16[128,768]{1,0:T(8,128)(2,1)} %reduce-scatter.3.cloned.1.call-done) | copy-start | bytes 589828
  179.4 11.2 %all-to-all-start.2 = ((bf16[8,24,384]{2,1,0:T(8,128)(2,1)}), bf16[8,24,384]{2,1,0:T(8,128)(2,1)S(1)}, u32[]{:S(2)}, u32[]{:S(2)}) async-start(bf16[8,24,384]{2,1,0:T(8,128)(2,1)} %all_to_all.93), calls=%async_computation.3 | async-start | bytes 294912 | tf_op jit(solution)/shard_map/all_to_all | solution.py:78
  182.8 88.2 %all-gather.13.cloned.1.call-start = ((), (), s32[]{:S(2)}) async-start(), calls=%async_computation.18 | async-start | bytes 1769472 | tf_op jit(solution)/shard_map/all_gather | solution.py:187
  184.9 0.8 copy-start.2
  184.9 3.6 %copy-start.29 = (f32[128]{0:T(128)}, f32[128]{0:T(128)S(1)}, u32[]{:S(2)}) copy-start(f32[128]{0:T(128)S(1)} %negate_multiply_fusion.1) | copy-start | bytes 1540
  190.7 6.2 %copy-start.9 = (bf16[128,768]{0,1:T(8,128)(2,1)S(1)}, bf16[128,768]{0,1:T(8,128)(2,1)}, u32[]{:S(2)}) copy-start(bf16[128,768]{0,1:T(8,128)(2,1)} %copy-done.8) | copy-start | bytes 589828
  191.8 5.4 %copy-start.7 = (bf16[128,768]{0,1:T(8,128)(2,1)S(1)}, bf16[128,768]{0,1:T(8,128)(2,1)}, u32[]{:S(2)}) copy-start(bf16[128,768]{0,1:T(8,128)(2,1)} %copy-done.6) | copy-start | bytes 589828
  191.8 18.8 %all-to-all-start.3 = ((bf16[4,192,768]{2,1,0:T(8,128)(2,1)}), bf16[4,192,768]{2,1,0:T(8,128)(2,1)}, u32[]{:S(2)}, u32[]{:S(2)}) async-start(bf16[4,192,768]{2,1,0:T(8,128)(2,1)} %broadcast_in_dim.34), calls=%async_computation.4 | async-start | bytes 2359296 | tf_op jit(solution)/shard_map/all_to_all | solution.py:78
  212.1 29.7 %all-to-all-start.4 = ((bf16[128,8,288]{0,2,1:T(8,128)(2,1)}), bf16[128,8,288]{0,2,1:T(8,128)(2,1)}, u32[]{:S(2)}, u32[]{:S(2)}) async-start(bf16[128,8,288]{0,2,1:T(8,128)(2,1)} %bitcast.108), calls=%async_computation.5 | async-start | bytes 1179648 | tf_op jit(solution)/shard_map/all_to_all | solution.py:78
  217.5 5.2 %copy-start.17 = (f32[768]{0:T(1024)S(1)}, f32[768]{0:T(1024)}, u32[]{:S(2)}) copy-start(f32[768]{0:T(1024)} %get-tuple-element.42) | copy-start | bytes 9220
  217.5 7.2 %copy-start.15 = (f32[12,64]{1,0:T(8,128)S(1)}, f32[12,64]{1,0:T(8,128)}, u32[]{:S(2)}) copy-start(f32[12,64]{1,0:T(8,128)} %get-tuple-element.62) | copy-start | bytes 9220
  241.8 6.2 %copy-start.19 = (f32[128]{0:T(128)S(1)}, f32[128]{0:T(128)}, u32[]{:S(2)}) copy-start(f32[128]{0:T(128)} %copy-done.18) | copy-start | bytes 1540
  241.8 24.1 %all-to-all-start.7 = ((bf16[128,8,96]{0,2,1:T(8,128)(2,1)}), bf16[128,8,96]{0,2,1:T(8,128)(2,1)}, u32[]{:S(2)}, u32[]{:S(2)}) async-start(bf16[128,8,96]{0,2,1:T(8,128)(2,1)} %bitcast.104), calls=%async_computation.9 | async-start | bytes 393216 | tf_op jit(solution)/shard_map/all_to_all | solution.py:78
  245.9 79.9 %reduce-scatter.5.cloned.1.call-start = ((), (), s32[]{:S(2)}) async-start(), calls=%async_computation.17 | async-start | bytes 1769472 | tf_op jit(solution)/shard_map/reduce_scatter | solution.py:209
  248.0 4.3 %copy-start.33 = (f32[128]{0:T(128)S(1)}, f32[128]{0:T(128)}, u32[]{:S(2)}) copy-start(f32[128]{0:T(128)} %copy-done.32) | copy-start | bytes 1540
  248.0 4.3 %copy-start.24 = (f32[128]{0:T(128)S(1)}, f32[128]{0:T(128)}, u32[]{:S(2)}) copy-start(f32[128]{0:T(128)} %copy-done.23) | copy-start | bytes 1540
  248.0 4.6 %copy-start.3 = (f32[128,768]{1,0:T(8,128)S(1)}, f32[128,768]{1,0:T(8,128)}, u32[]{:S(2)}) copy-start(f32[128,768]{1,0:T(8,128)} %copy-done.2) | copy-start | bytes 1179652
  248.0 4.6 %copy-start.12 = (bf16[128,768]{1,0:T(8,128)(2,1)S(1)}, bf16[128,768]{1,0:T(8,128)(2,1)}, u32[]{:S(2)}) copy-start(bf16[128,768]{1,0:T(8,128)(2,1)} %param.29) | copy-start | bytes 589828
  248.0 4.6 %copy-start.20 = (f32[128]{0:T(128)S(1)}, f32[128]{0:T(128)}, u32[]{:S(2)}) copy-start(f32[128]{0:T(128)} %copy-done.18) | copy-start | bytes 1540
  248.0 4.6 %copy-start.30 = (f32[128]{0:T(128)S(1)}, f32[128]{0:T(128)}, u32[]{:S(2)}) copy-start(f32[128]{0:T(128)} %copy-done.29) | copy-start | bytes 1540
  265.9 11.0 %all-to-all-start.5 = ((f32[8,1,768]{2,1,0:T(1,128)}), f32[8,1,768]{2,1,0:T(1,128)S(1)}, u32[]{:S(2)}, u32[]{:S(2)}) async-start(f32[8,1,768]{2,1,0:T(1,128)} %all_to_all.113), calls=%async_computation.7 | async-start | bytes 49152 | tf_op jit(solution)/shard_map/all_to_all | solution.py:78
  270.9 2.0 copy-start.10
  272.9 8.2 %copy-start.27 = (f32[384]{0:T(512)S(1)}, f32[384]{0:T(512)}, u32[]{:S(2)}) copy-start(f32[384]{0:T(512)} %get-tuple-element.51) | copy-start | bytes 4612
  276.9 13.3 %all-to-all-start.8 = ((bf16[4,96,768]{2,1,0:T(8,128)(2,1)}), bf16[4,96,768]{2,1,0:T(8,128)(2,1)}, u32[]{:S(2)}, u32[]{:S(2)}) async-start(bf16[4,96,768]{2,1,0:T(8,128)(2,1)} %pad_maximum_fusion.3), calls=%async_computation.10 | async-start | bytes 1179648 | tf_op jit(solution)/shard_map/all_to_all | solution.py:78
  290.9 7.9 %all-to-all-start.6 = ((f32[4,1,1152]{2,1,0:T(1,128)}), f32[4,1,1152]{2,1,0:T(1,128)S(1)}, u32[]{:S(2)}, u32[]{:S(2)}) async-start(f32[4,1,1152]{2,1,0:T(1,128)} %broadcast_in_dim.37), calls=%async_computation.8 | async-start | bytes 36864 | tf_op jit(solution)/shard_map/all_to_all | solution.py:78
  298.8 11.0 %all-to-all-start.9 = ((bf16[8,24,288]{2,1,0:T(8,128)(2,1)}), bf16[8,24,288]{2,1,0:T(8,128)(2,1)}, u32[]{:S(2)}, u32[]{:S(2)}) async-start(bf16[8,24,288]{2,1,0:T(8,128)(2,1)} %all_to_all.109), calls=%async_computation.11 | async-start | bytes 294912 | tf_op jit(solution)/shard_map/all_to_all | solution.py:78
  311.9 12.0 %all-to-all-start.10 = ((bf16[4,96,768]{2,1,0:T(8,128)(2,1)}), bf16[4,96,768]{2,1,0:T(8,128)(2,1)S(1)}, u32[]{:S(2)}, u32[]{:S(2)}) async-start(bf16[4,96,768]{2,1,0:T(8,128)(2,1)} %broadcast_in_dim.68), calls=%async_computation.12 | async-start | bytes 1179648 | tf_op jit(solution)/shard_map/all_to_all | solution.py:78
  324.0 1.9 copy-start.16
Sparse Core Ops, SparseCore 0:
  10.3 54.3 all-gather.6
  72.3 23.8 all-gather.8
  97.9 33.6 all-gather.10
  143.9 33.5 reduce-scatter.2
  179.1 25.0 all-gather.14
  206.2 34.6 all-gather.12
  249.1 35.6 reduce-scatter.4
